TPU v7x, 32 devices: a whole 2x2x4 slice. The times are simulated.
32 devices in a mesh: groups: 2 (over y), seq: 4 (over z), cell: 4 (over x, core).
Axes of the slice: x: 2, y: 2, z: 4, core: 2. Of those that a mesh axis runs over, the one named last changes fastest.
Arguments:
- dna_bases: int32 [65536], P(('groups', 'seq')), parts along dimension 0, may hold values from 0 to 3
- stem_weight: bfloat16 [512, 768], replicated, may hold values from -0.5 to 0.5
- conv_weight: bfloat16 [2, 384, 3, 768], P(None, 'cell'), may hold values from -0.125 to 0.125
- proj_weight: bfloat16 [2, 384, 768], P(None, 'cell'), may hold values from -0.3125 to 0.3125
- emission_head_weight: bfloat16 [32, 768, 128], P('cell'), may hold values from -0.046875 to 0.046875
- transitions: float32 [32, 128, 128], P('cell'), may hold values from -1 to 109
Outputs:
- log_marginals: float32 [32, 512, 128], P('cell', ('groups', 'seq')), parts along dimension 1
There are 2 independent parts, one for each index of `groups`. A program takes and returns all parts, laid end to end along the dimension named above; an argument that names none is the same for every part. Nothing has to cross between parts.
All inputs are finite; a program needn't handle non-finite values.
Results may differ from a plain program's by a relative error of at most 0.0007.
Values may be sent and summed in bfloat16 or wider, within the bound.
A program may use at most 128 MiB of HBM per device.

v0:
```python
import jax
import jax.numpy as jnp
from jax import lax
from jax.sharding import PartitionSpec as P

BIN_BP = 128
BASE_DILATION = 4


def with_halo(block, sides, width):
    for axis, dim in sides:
        count = lax.axis_size(axis)
        forward = [(i, i + 1) for i in range(count - 1)]
        backward = [(target, source) for source, target in forward]
        low = lax.ppermute(
            lax.slice_in_dim(block, block.shape[dim] - width, None, axis=dim), axis, forward
        )
        high = lax.ppermute(lax.slice_in_dim(block, 0, width, axis=dim), axis, backward)
        block = jnp.concatenate([low, block, high], axis=dim)
    return block


def prefix(value, axis, join, neutral, backward):
    count = lax.axis_size(axis)
    place = lax.axis_index(axis)
    ahead = count - 1 - place if backward else place
    gathered = lax.all_gather(value.astype(jnp.bfloat16), axis)
    state = jnp.zeros_like(value) + jnp.asarray(neutral, value.dtype)

    def one(lap, state):
        source = count - 1 - lap if backward else lap
        return join(state, lax.dynamic_index_in_dim(gathered, source, 0, False).astype(value.dtype))

    return lax.fori_loop(0, ahead, one, state)


def scaled(values):
    return values * lax.rsqrt(jnp.mean(values * values, axis=-1, keepdims=True) + 1e-06)


def tap_stack(conv_input, spacing_multiplier):
    out_rows = conv_input.shape[0] - 2 * spacing_multiplier
    return jnp.concatenate(
        [
            conv_input[0:out_rows],
            conv_input[spacing_multiplier : spacing_multiplier + out_rows],
            conv_input[2 * spacing_multiplier : 2 * spacing_multiplier + out_rows],
        ],
        axis=1,
    )


def mat_prod(left_mat, trailing_product):
    return jnp.einsum("crs,cst->crt", left_mat, trailing_product, precision=lax.Precision.HIGHEST)


def unit_peak(matrix):
    return matrix / jnp.max(matrix, axis=(-2, -1), keepdims=True)


def vec_peak(vector):
    return vector / jnp.max(vector, axis=-1, keepdims=True)


def forward_join(early_mat, late_mat):
    return unit_peak(mat_prod(early_mat, late_mat))


def backward_join(early_mat, late_mat):
    return unit_peak(mat_prod(late_mat, early_mat))


def branch(stacked, conv_slice, proj_slice):
    flat_weight = conv_slice.reshape(conv_slice.shape[0], -1)
    conv_out = lax.dot_general(
        stacked, flat_weight, (((1,), (1,)), ((), ())), preferred_element_type=jnp.float32
    )
    hidden = jax.nn.gelu(conv_out).astype(jnp.bfloat16)
    partial_value = jnp.dot(hidden, proj_slice, preferred_element_type=jnp.float32)
    return lax.psum(partial_value.astype(jnp.bfloat16), "cell").astype(jnp.float32)


def per_device(dna_bases, stem_weight, conv_weight, proj_weight, emission_head_weight, transitions):
    bin_rows = dna_bases.shape[0] // BIN_BP
    base_hits = dna_bases.reshape(bin_rows, BIN_BP, 1) == jnp.arange(4, dtype=jnp.int32)
    one_hot = base_hits.astype(jnp.bfloat16).reshape(bin_rows, BIN_BP * 4)
    stem_out = jnp.dot(one_hot, stem_weight, preferred_element_type=jnp.float32).astype(
        jnp.bfloat16
    )
    layers = conv_weight.shape[0]
    residual = stem_out.astype(jnp.float32)
    for layer_position in range(layers):
        spacing_multiplier = BASE_DILATION * 2**layer_position
        conv_input = jax.nn.gelu(scaled(residual)).astype(jnp.bfloat16)
        widened = with_halo(conv_input, (("seq", 0),), spacing_multiplier)
        residual = residual + branch(
            tap_stack(widened, spacing_multiplier),
            conv_weight[layer_position],
            proj_weight[layer_position],
        )
    trunk_features = scaled(residual).astype(jnp.bfloat16)
    emission_scores = jnp.einsum(
        "td,cds->cts", trunk_features, emission_head_weight, preferred_element_type=jnp.float32
    )
    cell_count = emission_scores.shape[0]
    state_count = emission_scores.shape[2]
    scaling = jnp.exp(emission_scores - jnp.max(emission_scores, axis=2, keepdims=True))
    trans_exp = jnp.exp(transitions - jnp.max(transitions, axis=(1, 2), keepdims=True))
    sub_len = 8
    sub_count = bin_rows // sub_len
    factors = scaling.reshape(cell_count, sub_count, sub_len, state_count)

    def block_product(inputs):
        transition_matrix, factor = inputs
        running_state = transition_matrix[None] * factor[:, 0, None, :]
        for position in range(1, sub_len):
            running_state = (
                jnp.einsum(
                    "ylv,vu->ylu", running_state, transition_matrix, precision=lax.Precision.HIGHEST
                )
                * factor[:, position, None, :]
            )
            running_state = unit_peak(running_state)
        combined = running_state
        for level_index in range(sub_count.bit_length() - 1):
            half_count = combined.shape[0] // 2
            paired_states = combined.reshape(half_count, 2, state_count, state_count)
            combined = unit_peak(
                jnp.einsum(
                    "mpw,mwy->mpy",
                    paired_states[:, 0],
                    paired_states[:, 1],
                    precision=lax.Precision.HIGHEST,
                )
            )
        return (running_state, combined[0])

    segment_list, block = lax.map(block_product, (trans_exp, factors))
    identity = jnp.broadcast_to(jnp.eye(state_count, dtype=jnp.float32), block.shape)
    prefix_mat = prefix(block, "seq", forward_join, identity, False)
    suffix_mat = prefix(block, "seq", backward_join, identity, True)
    enter_vec = vec_peak(jnp.sum(prefix_mat, axis=1))
    leave_vec = vec_peak(jnp.sum(suffix_mat, axis=2))
    chain_pieces = jnp.swapaxes(segment_list, 0, 1)

    def forward_step(vector, piece_mat):
        return (
            vec_peak(jnp.einsum("cr,crs->cs", vector, piece_mat, precision=lax.Precision.HIGHEST)),
            vector,
        )

    def backward_step(vector, piece_mat):
        return (
            vec_peak(jnp.einsum("crs,cs->cr", piece_mat, vector, precision=lax.Precision.HIGHEST)),
            vector,
        )

    _, starts = lax.scan(forward_step, enter_vec, chain_pieces)
    _, after_vecs = lax.scan(backward_step, leave_vec, chain_pieces, reverse=True)
    vector = jnp.swapaxes(starts, 0, 1)
    forward_list = []
    for position in range(sub_len):
        vector = vec_peak(
            jnp.einsum("cgr,crs->cgs", vector, trans_exp, precision=lax.Precision.HIGHEST)
            * factors[:, :, position]
        )
        forward_list.append(vector)
    vector = jnp.swapaxes(after_vecs, 0, 1)
    backward_list = [vector] * sub_len
    for position in range(sub_len - 1, -1, -1):
        backward_list[position] = vector
        if position > 0:
            vector = vec_peak(
                jnp.einsum(
                    "crs,cgs->cgr",
                    trans_exp,
                    factors[:, :, position] * vector,
                    precision=lax.Precision.HIGHEST,
                )
            )
    alpha_all = jnp.stack(forward_list, axis=2).reshape(cell_count, bin_rows, state_count)
    beta_all = jnp.stack(backward_list, axis=2).reshape(cell_count, bin_rows, state_count)
    joint_log = jnp.log(alpha_all) + jnp.log(beta_all)
    return jnp.maximum(joint_log - jax.nn.logsumexp(joint_log, axis=2, keepdims=True), -30.0)


def solution(mesh):
    placed = (
        P(("groups", "seq")),
        P(),
        P(None, "cell", None, None),
        P(None, "cell", None),
        P("cell", None, None),
        P("cell", None, None),
    )
    return jax.shard_map(
        per_device,
        mesh=mesh,
        in_specs=placed,
        out_specs=P("cell", ("groups", "seq"), None),
        check_vma=False,
    )
```

profile of v0, /device:TPU:0, one launch (start us, length us, event | category | flops | bytes accessed | tf_op | source)
XLA Modules:
  0.0 269.2 jit_solution(5592147471232159884)
XLA Ops:
  7.7 1.7 multiply_reduce_fusion.2
  9.5 5.0 %collective-permute-start = (bf16[4,768]{1,0:T(4,128)(2,1)S(1)}, bf16[4,768]{1,0:T(4,128)(2,1)S(1)}, u32[]{:S(2)}, u32[]{:S(2)}) collective-permute-start(bf16[4,768]{1,0:T(4,128)(2,1)S(1)} %get-tuple-element.359), channel_id=1, source_target_pairs={{0,4},{4,8},{8,12},{1,5},{5,9},{9,13},{2,6},{6,10},{10,14},{3,7},{... | collective-permute-start | bytes 18440 | tf_op jit(solution)/shard_map/ppermute | solution.py:15
  17.6 2.6 collective-permute-done.1
  20.2 2.0 convolution_convert_fusion.2
  22.3 32.0 %all-reduce.3.cloned.1.call-done = bf16[64,768]{1,0:T(8,128)(2,1)} async-done(((bf16[64,768]{1,0:T(8,128)(2,1)}), bf16[64,768]{1,0:T(8,128)(2,1)}) %all-reduce.3.cloned.1.call-update) | async-done | bytes 98320 | tf_op jit(solution)/shard_map/psum | solution.py:80
  56.5 3.4 %collective-permute-start.2 = (bf16[8,768]{1,0:T(8,128)(2,1)S(1)}, bf16[8,768]{1,0:T(8,128)(2,1)S(1)}, u32[]{:S(2)}, u32[]{:S(2)}) collective-permute-start(bf16[8,768]{1,0:T(8,128)(2,1)S(1)} %get-tuple-element.357), channel_id=1, source_target_pairs={{0,4},{4,8},{8,12},{1,5},{5,9},{9,13},{2,6},{6,10},{10,14},{3,7},{... | collective-permute-start | bytes 36872 | tf_op jit(solution)/shard_map/ppermute | solution.py:15
  61.8 3.7 %collective-permute-done.3 = bf16[8,768]{1,0:T(8,128)(2,1)S(1)} collective-permute-done((bf16[8,768]{1,0:T(8,128)(2,1)S(1)}, bf16[8,768]{1,0:T(8,128)(2,1)S(1)}, u32[]{:S(2)}, u32[]{:S(2)}) %collective-permute-start.3) | collective-permute-done | bytes 12320 | tf_op jit(solution)/shard_map/ppermute | solution.py:18
  65.5 2.0 convolution_convert_fusion.1
  67.7 30.7 %all-reduce.5.cloned.1.call-done = bf16[64,768]{1,0:T(8,128)(2,1)} async-done(((bf16[64,768]{1,0:T(8,128)(2,1)}), bf16[64,768]{1,0:T(8,128)(2,1)}) %all-reduce.5.cloned.1.call-update) | async-done | bytes 98320 | tf_op jit(solution)/shard_map/psum | solution.py:80
  100.9 73.1 %while.62 = (s32[]{:T(128)}, f32[8,8,128,128]{3,2,0,1:T(8,128)}, bf16[8,128,128]{2,1,0:T(8,128)(2,1)}, f32[8,128,128]{2,1,0:T(8,128)S(1)}, f32[8,8,8,128]{3,2,1,0:T(8,128)S(1)}, /*index=5*/s32[]{:T(128)}) while((s32[]{:T(128)}, f32[8,8,128,128]{3,2,0,1:T(8,128)}, bf16[8,128,128]{2,1,0:T(8,128)(2,1)}, f32[8,128,128]{2,1,0:T(8,128)S(1)}, ...), condition=%wide.region_18.19_spmd, body=%wide.region_7.18_spmd.sunk | while | flops 1588559872 | bytes 11572125 | solution.py:138
  174.3 27.8 %all-gather.3.cloned.1.call-done = bf16[32,128,128]{2,1,0:T(8,128)(2,1)} async-done(((bf16[8,128,128]{2,1,0:T(8,128)(2,1)}), bf16[32,128,128]{2,1,0:T(8,128)(2,1)}) %all-gather.3.cloned.1.call-update) | async-done | bytes 1048592 | tf_op jit(solution)/shard_map/all_gather | solution.py:27
  202.6 14.4 %while.64 = (s32[]{:T(128)}, f32[8,128]{1,0:T(8,128)S(1)}, f32[8,8,128]{2,1,0:T(8,128)S(1)}, f32[8,8,128,128]{3,2,1,0:T(8,128)}, s32[]{:T(128)}, /*index=5*/f32[]{:T(128)}) while((s32[]{:T(128)}, f32[8,128]{1,0:T(8,128)S(1)}, f32[8,8,128]{2,1,0:T(8,128)S(1)}, f32[8,8,128,128]{3,2,1,0:T(8,128)}, s32[]{:T(128)}, /*index=5*/f32[]{:T(128)}) %tuple.192), condition=%wide.region_26.27_spmd, body=%wide.region_24.26_spmd.sunk | while | flops 1574906 | bytes 553613 | solution.py:158
  202.6 1.6 fusion.296
  204.4 1.6 fusion.296
  206.2 1.6 fusion.296
  208.0 1.6 fusion.296
  209.8 1.6 fusion.296
  211.6 1.6 fusion.296
  213.4 1.6 fusion.296
  215.2 1.6 fusion.296
  218.3 5.0 %while.65 = (s32[]{:T(128)}, f32[8,128,128]{2,1,0:T(8,128)S(1)}, s32[]{:T(128)}, bf16[4,8,128,128]{3,2,1,0:T(8,128)(2,1)}, s32[]{:T(128)}, /*index=5*/s32[]{:T(128)}, s32[]{:T(128)}, s32[]{:T(128)}) while((s32[]{:T(128)}, f32[8,128,128]{2,1,0:T(8,128)S(1)}, s32[]{:T(128)}, bf16[4,8,128,128]{3,2,1,0:T(8,128)(2,1)}, s32[]{:T(128)}, ...), condition=%wide.region_37.38_spmd, body=%wide.region_35.37_spmd.sunk | while | flops 201588736 | bytes 2359495 | solution.py:34
  219.9 1.4 fusion.298
  221.5 1.4 fusion.298
  223.7 17.6 %while.66 = (s32[]{:T(128)}, f32[8,128]{1,0:T(8,128)S(1)}, f32[8,8,128]{2,0,1:T(8,128)S(1)}, f32[8,8,128,128]{3,2,1,0:T(8,128)}, s32[]{:T(128)}, /*index=5*/s32[]{:T(128)}, f32[]{:T(128)}, s32[]{:T(128)}) while((s32[]{:T(128)}, f32[8,128]{1,0:T(8,128)S(1)}, f32[8,8,128]{2,0,1:T(8,128)S(1)}, f32[8,8,128,128]{3,2,1,0:T(8,128)}, s32[]{:T(128)}, ...), condition=%wide.region_42.43_spmd, body=%wide.region_40.42_spmd.sunk | while | flops 1574907 | bytes 553133 | solution.py:159
  223.7 2.0 fusion.301
  225.9 2.0 fusion.301
  228.1 2.0 fusion.301
  230.3 2.0 fusion.301
  232.5 2.0 fusion.301
  234.7 2.0 fusion.301
  236.9 2.0 fusion.301
  239.1 2.0 fusion.301
  (296 shorter events, 112.7 us)
Async XLA Ops:
  6.5 92.9 %copy-start = (bf16[8,768,128]{2,1,0:T(8,128)(2,1)S(1)}, bf16[8,768,128]{2,1,0:T(8,128)(2,1)}, u32[]{:S(2)}) copy-start(bf16[8,768,128]{2,1,0:T(8,128)(2,1)} %param.20) | copy-start | bytes 4718596
  6.5 47.8 %all-reduce.3.cloned.1.call-start = ((), (), s32[]{:S(2)}) async-start(), calls=%async_computation | async-start | bytes 196608 | tf_op jit(solution)/shard_map/psum | solution.py:80
  9.5 8.1 %collective-permute-start = (bf16[4,768]{1,0:T(4,128)(2,1)S(1)}, bf16[4,768]{1,0:T(4,128)(2,1)S(1)}, u32[]{:S(2)}, u32[]{:S(2)}) collective-permute-start(bf16[4,768]{1,0:T(4,128)(2,1)S(1)} %get-tuple-element.359), channel_id=1, source_target_pairs={{0,4},{4,8},{8,12},{1,5},{5,9},{9,13},{2,6},{6,10},{10,14},{3,7},{... | collective-permute-start | bytes 18440 | tf_op jit(solution)/shard_map/ppermute | solution.py:15
  14.5 47.1 %copy-start.1 = (f32[8,128,128]{2,1,0:T(8,128)S(1)}, f32[8,128,128]{2,1,0:T(8,128)}, u32[]{:S(2)}) copy-start(f32[8,128,128]{2,1,0:T(8,128)} %param.21) | copy-start | bytes 1572868
  14.5 5.7 %collective-permute-start.1 = (bf16[4,768]{1,0:T(4,128)(2,1)S(1)}, bf16[4,768]{1,0:T(4,128)(2,1)S(1)}, u32[]{:S(2)}, u32[]{:S(2)}) collective-permute-start(bf16[4,768]{1,0:T(4,128)(2,1)S(1)} %get-tuple-element.360), channel_id=1, source_target_pairs={{4,0},{8,4},{12,8},{5,1},{9,5},{13,9},{6,2},{10,6},{14,10},{7,3},{... | collective-permute-start | bytes 18440 | tf_op jit(solution)/shard_map/ppermute | solution.py:18
  22.2 76.2 %all-reduce.5.cloned.1.call-start = ((), (), s32[]{:S(2)}) async-start(), calls=%async_computation.1 | async-start | bytes 196608 | tf_op jit(solution)/shard_map/psum | solution.py:80
  54.3 44.1 %copy-start.2 = (bf16[64,768]{1,0:T(8,128)(2,1)S(1)}, bf16[64,768]{1,0:T(8,128)(2,1)}, u32[]{:S(2)}) copy-start(bf16[64,768]{1,0:T(8,128)(2,1)} %all-reduce.3.cloned.1.call-done) | copy-start | bytes 294916
  56.5 5.3 %collective-permute-start.2 = (bf16[8,768]{1,0:T(8,128)(2,1)S(1)}, bf16[8,768]{1,0:T(8,128)(2,1)S(1)}, u32[]{:S(2)}, u32[]{:S(2)}) collective-permute-start(bf16[8,768]{1,0:T(8,128)(2,1)S(1)} %get-tuple-element.357), channel_id=1, source_target_pairs={{0,4},{4,8},{8,12},{1,5},{5,9},{9,13},{2,6},{6,10},{10,14},{3,7},{... | collective-permute-start | bytes 36872 | tf_op jit(solution)/shard_map/ppermute | solution.py:15
  59.9 5.6 %collective-permute-start.3 = (bf16[8,768]{1,0:T(8,128)(2,1)S(1)}, bf16[8,768]{1,0:T(8,128)(2,1)S(1)}, u32[]{:S(2)}, u32[]{:S(2)}) collective-permute-start(bf16[8,768]{1,0:T(8,128)(2,1)S(1)} %get-tuple-element.358), channel_id=1, source_target_pairs={{4,0},{8,4},{12,8},{5,1},{9,5},{13,9},{6,2},{10,6},{14,10},{7,3},{... | collective-permute-start | bytes 36872 | tf_op jit(solution)/shard_map/ppermute | solution.py:18
  67.5 134.7 %all-gather.3.cloned.1.call-start = ((), (), s32[]{:S(2)}) async-start(), calls=%async_computation.2 | async-start | bytes 1310720 | tf_op jit(solution)/shard_map/all_gather | solution.py:27
Sparse Core Ops, SparseCore 0:
  22.4 31.9 all-reduce.2
  67.6 30.7 all-reduce.4
  174.1 27.9 all-gather.2
where the time goes:
time: 271 us; the launch traced here: 269 us
  matrix products  104 us (38%)
  waiting for transfers between devices  96.8 us (36%)
  other arithmetic  37.8 us (14%)
  between operations  13.5 us (5%)
  starting transfers between devices  11.1 us (4%)
  local copies, waits for them, and re-layouts  4.66 us (2%)
    psum x2, waiting for transfers between devices, branch(): lax.psum(partial_value.astype(jnp.bfloat16), 'cell').astype(jnp.float32)  62.7 us
    dot_general x56, matrix products, block_product(): jnp.einsum('ylv,vu->ylu', running_state, transition_matrix, precision=lax...  40 us
    all_gather x1, waiting for transfers between devices, prefix(): gathered = lax.all_gather(value.astype(jnp.bfloat16), axis)  27.8 us
    dynamic_update_slice x16, other arithmetic, per_device(): segment_list, block = lax.map(block_product, (trans_exp, factors))  17.7 us
    dot_general x8, matrix products, backward_step(): jnp.einsum('crs,cs->cr', piece_mat, vector, precision=lax.Precision.HIGHEST)  15.7 us
    dot_general x24, matrix products, block_product(): jnp.einsum('mpw,mwy->mpy', paired_states[:, 0], paired_states[:, 1], prec...  13.3 us
    dot_general x8, matrix products, forward_step(): jnp.einsum('cr,crs->cs', vector, piece_mat, precision=lax.Precision.HIGHEST)  12.8 us
    div x33, other arithmetic, vec_peak(): return vector / jnp.max(vector, axis=-1, keepdims=True)  10.7 us
  transfers between devices with their start and end apart: 7, of which 5 were waited for; matrix products, arithmetic and copies ran while one was open for 1% of the time, Pallas kernels for 0%

commit v1 on v0

--- a/solution.py
+++ b/solution.py
@@ -1,3 +1,4 @@
+import functools
 import jax
 import jax.numpy as jnp
 from jax import lax
@@ -5,6 +6,13 @@
 
 BIN_BP = 128
 BASE_DILATION = 4
+
+
+def pair_stops_all(page, axis_tag):
+    return jnp.sum(lax.all_gather(page, axis_tag), axis=0)
+
+
+update_shards_here = functools.partial(pair_stops_all, axis_tag="cell")
 
 
 def with_halo(block, sides, width):
@@ -77,7 +85,7 @@
     )
     hidden = jax.nn.gelu(conv_out).astype(jnp.bfloat16)
     partial_value = jnp.dot(hidden, proj_slice, preferred_element_type=jnp.float32)
-    return lax.psum(partial_value.astype(jnp.bfloat16), "cell").astype(jnp.float32)
+    return update_shards_here(partial_value.astype(jnp.bfloat16)).astype(jnp.float32)
 
 
 def per_device(dna_bases, stem_weight, conv_weight, proj_weight, emission_head_weight, transitions):

time: 271 us -> 214 us (0.79)
  waiting for transfers between devices: 96.8 us -> 32.8 us
  blocking collectives: 0 us -> 12.6 us
    psum x2 -> x0, waiting for transfers between devices: 62.7 us -> none  [branch(): lax.psum(partial_value.astype(jnp.bfloat16), 'cell').astype(jnp.float32)]
    all_gather x0 -> x2, blocking collectives: none -> 12.6 us  [pair_stops_all(): return jnp.sum(lax.all_gather(page, axis_tag), axis=0)]
  transfers between devices with their start and end apart: 7 -> 5, of which waited for: 5 -> 3; matrix products, arithmetic and copies ran while one was open for 1% -> 1% of each run, Pallas kernels for 0% -> 0%
where the time goes in v1:
time: 214 us; the launch traced here: 213 us
  matrix products  102 us (48%)
  other arithmetic  35.2 us (16%)
  waiting for transfers between devices  32.8 us (15%)
  between operations  13.8 us (6%)
  blocking collectives  12.6 us (6%)
  starting transfers between devices  11 us (5%)
  local copies, waits for them, and re-layouts  4.68 us (2%)
    dot_general x56, matrix products, block_product(): jnp.einsum('ylv,vu->ylu', running_state, transition_matrix, precision=lax...  40 us
    all_gather x1, waiting for transfers between devices, prefix(): gathered = lax.all_gather(value.astype(jnp.bfloat16), axis)  26.7 us
    dynamic_update_slice x16, other arithmetic, per_device(): segment_list, block = lax.map(block_product, (trans_exp, factors))  17.7 us
    dot_general x8, matrix products, backward_step(): jnp.einsum('crs,cs->cr', piece_mat, vector, precision=lax.Precision.HIGHEST)  15.7 us
    dot_general x24, matrix products, block_product(): jnp.einsum('mpw,mwy->mpy', paired_states[:, 0], paired_states[:, 1], prec...  13.3 us
    dot_general x8, matrix products, forward_step(): jnp.einsum('cr,crs->cs', vector, piece_mat, precision=lax.Precision.HIGHEST)  12.8 us
    all_gather x2, blocking collectives, pair_stops_all(): return jnp.sum(lax.all_gather(page, axis_tag), axis=0)  12.6 us
    div x33, other arithmetic, vec_peak(): return vector / jnp.max(vector, axis=-1, keepdims=True)  10.7 us
  transfers between devices with their start and end apart: 5, of which 3 were waited for; matrix products, arithmetic and copies ran while one was open for 1% of the time, Pallas kernels for 0%

profile of v1, /device:TPU:0, one launch (start us, length us, event | category | flops | bytes accessed | tf_op | source)
XLA Modules:
  0.0 213.1 jit_solution(11532496796395993112)
XLA Ops:
  7.7 1.7 multiply_reduce_fusion.2
  9.6 5.0 %collective-permute-start = (bf16[4,768]{1,0:T(4,128)(2,1)S(1)}, bf16[4,768]{1,0:T(4,128)(2,1)S(1)}, u32[]{:S(2)}, u32[]{:S(2)}) collective-permute-start(bf16[4,768]{1,0:T(4,128)(2,1)S(1)} %get-tuple-element.359), channel_id=1, source_target_pairs={{0,4},{4,8},{8,12},{1,5},{5,9},{9,13},{2,6},{6,10},{10,14},{3,7},{... | collective-permute-start | bytes 18440 | tf_op jit(solution)/shard_map/ppermute | solution.py:23
  17.7 2.4 %collective-permute-done.1 = bf16[4,768]{1,0:T(4,128)(2,1)S(1)} collective-permute-done((bf16[4,768]{1,0:T(4,128)(2,1)S(1)}, bf16[4,768]{1,0:T(4,128)(2,1)S(1)}, u32[]{:S(2)}, u32[]{:S(2)}) %collective-permute-start.1) | collective-permute-done | bytes 6176 | tf_op jit(solution)/shard_map/ppermute | solution.py:26
  20.1 1.4 convolution_convert_fusion.2
  21.5 6.5 %all-gather = bf16[256,768]{1,0:T(8,128)(2,1)S(1)} all-gather(bf16[64,768]{1,0:T(8,128)(2,1)S(1)} %convolution_convert_fusion.2), channel_id=2, replica_groups=mesh['groups'=2,'seq'=4,'cell'=4] {'cell'}, dimensions={0}, use_global_device_ids=true | all-gather | bytes 491520 | tf_op jit(solution)/shard_map/all_gather | solution.py:12
  28.3 3.5 %collective-permute-start.2 = (bf16[8,768]{1,0:T(8,128)(2,1)S(1)}, bf16[8,768]{1,0:T(8,128)(2,1)S(1)}, u32[]{:S(2)}, u32[]{:S(2)}) collective-permute-start(bf16[8,768]{1,0:T(8,128)(2,1)S(1)} %get-tuple-element.357), channel_id=1, source_target_pairs={{0,4},{4,8},{8,12},{1,5},{5,9},{9,13},{2,6},{6,10},{10,14},{3,7},{... | collective-permute-start | bytes 36872 | tf_op jit(solution)/shard_map/ppermute | solution.py:23
  33.7 3.7 %collective-permute-done.3 = bf16[8,768]{1,0:T(8,128)(2,1)S(1)} collective-permute-done((bf16[8,768]{1,0:T(8,128)(2,1)S(1)}, bf16[8,768]{1,0:T(8,128)(2,1)S(1)}, u32[]{:S(2)}, u32[]{:S(2)}) %collective-permute-start.3) | collective-permute-done | bytes 12320 | tf_op jit(solution)/shard_map/ppermute | solution.py:26
  38.7 6.1 %all-gather.1 = bf16[256,768]{1,0:T(8,128)(2,1)S(1)} all-gather(bf16[64,768]{1,0:T(8,128)(2,1)S(1)} %convolution_convert_fusion.1), channel_id=3, replica_groups=mesh['groups'=2,'seq'=4,'cell'=4] {'cell'}, dimensions={0}, use_global_device_ids=true | all-gather | bytes 491520 | tf_op jit(solution)/shard_map/all_gather | solution.py:12
  45.7 73.1 %while.62 = (s32[]{:T(128)}, f32[8,8,128,128]{3,2,0,1:T(8,128)}, bf16[8,128,128]{2,1,0:T(8,128)(2,1)}, f32[8,128,128]{2,1,0:T(8,128)S(1)}, f32[8,8,8,128]{3,2,1,0:T(8,128)S(1)}, /*index=5*/s32[]{:T(128)}) while((s32[]{:T(128)}, f32[8,8,128,128]{3,2,0,1:T(8,128)}, bf16[8,128,128]{2,1,0:T(8,128)(2,1)}, f32[8,128,128]{2,1,0:T(8,128)S(1)}, ...), condition=%wide.region_18.19_spmd, body=%wide.region_7.18_spmd.sunk | while | flops 1588559872 | bytes 11572125 | solution.py:146
  119.1 26.7 %all-gather.5.cloned.1.call-done = bf16[32,128,128]{2,1,0:T(8,128)(2,1)} async-done(((bf16[8,128,128]{2,1,0:T(8,128)(2,1)}), bf16[32,128,128]{2,1,0:T(8,128)(2,1)}) %all-gather.5.cloned.1.call-update) | async-done | bytes 1048592 | tf_op jit(solution)/shard_map/all_gather | solution.py:35
  146.3 14.4 %while.64 = (s32[]{:T(128)}, f32[8,128]{1,0:T(8,128)S(1)}, f32[8,8,128]{2,1,0:T(8,128)S(1)}, f32[8,8,128,128]{3,2,1,0:T(8,128)}, s32[]{:T(128)}, /*index=5*/f32[]{:T(128)}) while((s32[]{:T(128)}, f32[8,128]{1,0:T(8,128)S(1)}, f32[8,8,128]{2,1,0:T(8,128)S(1)}, f32[8,8,128,128]{3,2,1,0:T(8,128)}, s32[]{:T(128)}, /*index=5*/f32[]{:T(128)}) %tuple.188), condition=%wide.region_26.27_spmd, body=%wide.region_24.26_spmd.sunk | while | flops 1574906 | bytes 553613 | solution.py:166
  146.3 1.6 fusion.296
  148.1 1.6 fusion.296
  149.9 1.6 fusion.296
  151.7 1.6 fusion.296
  153.5 1.6 fusion.296
  155.3 1.6 fusion.296
  157.1 1.6 fusion.296
  158.9 1.6 fusion.296
  161.9 5.0 %while.65 = (s32[]{:T(128)}, f32[8,128,128]{2,1,0:T(8,128)S(1)}, s32[]{:T(128)}, bf16[4,8,128,128]{3,2,1,0:T(8,128)(2,1)}, s32[]{:T(128)}, /*index=5*/s32[]{:T(128)}, s32[]{:T(128)}, s32[]{:T(128)}) while((s32[]{:T(128)}, f32[8,128,128]{2,1,0:T(8,128)S(1)}, s32[]{:T(128)}, bf16[4,8,128,128]{3,2,1,0:T(8,128)(2,1)}, s32[]{:T(128)}, ...), condition=%wide.region_37.38_spmd, body=%wide.region_35.37_spmd.sunk | while | flops 201588736 | bytes 2359495 | solution.py:42
  162.0 1.4 fusion.298
  163.6 1.4 fusion.298
  165.2 1.4 fusion.298
  167.3 17.6 %while.66 = (s32[]{:T(128)}, f32[8,128]{1,0:T(8,128)S(1)}, f32[8,8,128]{2,0,1:T(8,128)S(1)}, f32[8,8,128,128]{3,2,1,0:T(8,128)}, s32[]{:T(128)}, /*index=5*/s32[]{:T(128)}, f32[]{:T(128)}, s32[]{:T(128)}) while((s32[]{:T(128)}, f32[8,128]{1,0:T(8,128)S(1)}, f32[8,8,128]{2,0,1:T(8,128)S(1)}, f32[8,8,128,128]{3,2,1,0:T(8,128)}, s32[]{:T(128)}, ...), condition=%wide.region_42.43_spmd, body=%wide.region_40.42_spmd.sunk | while | flops 1574907 | bytes 553133 | solution.py:167
  167.3 2.0 fusion.301
  169.5 2.0 fusion.301
  171.7 2.0 fusion.301
  173.9 2.0 fusion.301
  176.1 2.0 fusion.301
  178.3 2.0 fusion.301
  180.6 2.0 fusion.301
  182.8 2.0 fusion.301
  (292 shorter events, 108.9 us)
Async XLA Ops:
  6.5 38.6 %copy-start = (bf16[8,768,128]{2,1,0:T(8,128)(2,1)S(1)}, bf16[8,768,128]{2,1,0:T(8,128)(2,1)}, u32[]{:S(2)}) copy-start(bf16[8,768,128]{2,1,0:T(8,128)(2,1)} %param.20) | copy-start | bytes 4718596
  6.5 11.0 %copy-start.1 = (f32[8,128,128]{2,1,0:T(8,128)S(1)}, f32[8,128,128]{2,1,0:T(8,128)}, u32[]{:S(2)}) copy-start(f32[8,128,128]{2,1,0:T(8,128)} %param.21) | copy-start | bytes 1572868
  6.5 139.3 %all-gather.5.cloned.1.call-start = ((), (), s32[]{:S(2)}) async-start(), calls=%async_computation | async-start | bytes 1310720 | tf_op jit(solution)/shard_map/all_gather | solution.py:35
  9.6 8.1 %collective-permute-start = (bf16[4,768]{1,0:T(4,128)(2,1)S(1)}, bf16[4,768]{1,0:T(4,128)(2,1)S(1)}, u32[]{:S(2)}, u32[]{:S(2)}) collective-permute-start(bf16[4,768]{1,0:T(4,128)(2,1)S(1)} %get-tuple-element.359), channel_id=1, source_target_pairs={{0,4},{4,8},{8,12},{1,5},{5,9},{9,13},{2,6},{6,10},{10,14},{3,7},{... | collective-permute-start | bytes 18440 | tf_op jit(solution)/shard_map/ppermute | solution.py:23
  14.5 5.5 %collective-permute-start.1 = (bf16[4,768]{1,0:T(4,128)(2,1)S(1)}, bf16[4,768]{1,0:T(4,128)(2,1)S(1)}, u32[]{:S(2)}, u32[]{:S(2)}) collective-permute-start(bf16[4,768]{1,0:T(4,128)(2,1)S(1)} %get-tuple-element.360), channel_id=1, source_target_pairs={{4,0},{8,4},{12,8},{5,1},{9,5},{13,9},{6,2},{10,6},{14,10},{7,3},{... | collective-permute-start | bytes 18440 | tf_op jit(solution)/shard_map/ppermute | solution.py:26
  28.3 5.4 %collective-permute-start.2 = (bf16[8,768]{1,0:T(8,128)(2,1)S(1)}, bf16[8,768]{1,0:T(8,128)(2,1)S(1)}, u32[]{:S(2)}, u32[]{:S(2)}) collective-permute-start(bf16[8,768]{1,0:T(8,128)(2,1)S(1)} %get-tuple-element.357), channel_id=1, source_target_pairs={{0,4},{4,8},{8,12},{1,5},{5,9},{9,13},{2,6},{6,10},{10,14},{3,7},{... | collective-permute-start | bytes 36872 | tf_op jit(solution)/shard_map/ppermute | solution.py:23
  31.8 5.6 %collective-permute-start.3 = (bf16[8,768]{1,0:T(8,128)(2,1)S(1)}, bf16[8,768]{1,0:T(8,128)(2,1)S(1)}, u32[]{:S(2)}, u32[]{:S(2)}) collective-permute-start(bf16[8,768]{1,0:T(8,128)(2,1)S(1)} %get-tuple-element.358), channel_id=1, source_target_pairs={{4,0},{8,4},{12,8},{5,1},{9,5},{13,9},{6,2},{10,6},{14,10},{7,3},{... | collective-permute-start | bytes 36872 | tf_op jit(solution)/shard_map/ppermute | solution.py:26
Sparse Core Ops, SparseCore 0:
  118.9 26.8 all-gather.4
